TPU v7x, 32 devices: a whole 2x2x4 slice. The times are simulated.
32 devices in a mesh: row: 8 (over y, x, core), col: 4 (over z).
Axes of the slice: x: 2, y: 2, z: 4, core: 2. Of those that a mesh axis runs over, the one named last changes fastest.
Arguments:
- hidden_in: bfloat16 [1152, 2048], P('col', 'row'), may hold values from -21 to 21
- state: float32 [128, 2048, 1152], P('col', 'row'), may hold values from -4 to 4
- attn_norm_gain: bfloat16 [2048], replicated, may hold values from 0.099609375 to 1.8984375
- w_query: bfloat16 [2048, 2048], P(None, 'row'), may hold values from -0.125 to 0.125
- w_key: bfloat16 [2048, 2048], P(None, 'row'), may hold values from -0.125 to 0.125
- w_value: bfloat16 [2048, 2048], P(None, 'row'), may hold values from -0.125 to 0.125
- w_gate: bfloat16 [2048, 2048], P(None, 'row'), may hold values from -0.125 to 0.125
- w_decay: bfloat16 [2048, 16], replicated, may hold values from -0.125 to 0.125
- w_beta: bfloat16 [2048, 16], replicated, may hold values from -0.125 to 0.125
- decay_log: float32 [16], replicated, may hold values from -3 to 1.5
- decay_bias: float32 [16], replicated, may hold values from -2 to 1
- head_gain: float32 [128], replicated, may hold values from 0.1 to 1.9
- w_out: bfloat16 [2048, 2048], P('row'), may hold values from -0.125 to 0.125
- final_gain: bfloat16 [2048], P('row'), may hold values from 0.099609375 to 1.8984375
- lm_weight: bfloat16 [2048, 20480], P(None, ('row', 'col')), may hold values from -0.28726213 to 0.28726213
- token_ids: int32 [1152], replicated, may hold values from 0 to 20479
- ref_logprob: float32 [1152], replicated, may hold values from -16 to -6
Outputs:
- new_state: float32 [128, 2048, 1152], P('col', 'row')
- logprob: float32 [1152], replicated
- entropy: float32 [1152], replicated
- kl: float32 [1152], replicated
All inputs are finite; a program needn't handle non-finite values.
Results may differ from a plain program's by a relative error of at most 0.0014.
The roundings to bfloat16 on the way count: a program that leaves them out, or rounds other values in their place, can miss the bound.
Values may be sent and summed in bfloat16 or wider, within the bound.
A program may use at most 128 MiB of HBM per device.

v0:
```python
import jax
import jax.numpy as jnp
from jax import lax
from jax.sharding import PartitionSpec as P

D = 2048
HEADS = 16
DK = 128
DV = 128


def partner_2(block, axis, apart):
    count = lax.axis_size(axis)
    route = []
    for low in range(count):
        high = low | 1 << apart
        if high != low and high < count:
            route += [(low, high), (high, low)]
    return lax.ppermute(block, axis, route)


def project(weight, normed):
    return lax.dot_general(
        weight, normed, (((0,), (1,)), ((), ())), preferred_element_type=jnp.float32
    )


def shift_pairs(count, step):
    return [(source, (source + step) % count) for source in range(count)]


def swap_blocks(blocks, axis):
    count = lax.axis_size(axis)
    me = lax.axis_index(axis)
    result = blocks
    for step in range(1, count):
        sent = lax.dynamic_index_in_dim(blocks, (me + step) % count, 0, keepdims=True)
        got = lax.ppermute(sent, axis, shift_pairs(count, step))
        result = lax.dynamic_update_slice_in_dim(result, got, (me - step) % count, 0)
    return result


def gather_blocks(block, axis):
    count = lax.axis_size(axis)
    me = lax.axis_index(axis)
    result = jnp.zeros((count,) + block.shape, block.dtype)
    result = lax.dynamic_update_slice_in_dim(result, block[None], me, 0)
    for step in range(1, count):
        got = lax.ppermute(block[None], axis, shift_pairs(count, step))
        result = lax.dynamic_update_slice_in_dim(result, got, (me - step) % count, 0)
    return result


def sum_blocks(blocks, axis):
    count = lax.axis_size(axis)
    me = lax.axis_index(axis)
    total = lax.dynamic_index_in_dim(blocks, me, 0, keepdims=False)
    for step in range(1, count):
        sent = lax.dynamic_index_in_dim(blocks, (me + step) % count, 0, keepdims=False)
        total = total + lax.ppermute(sent, axis, shift_pairs(count, step))
    return total


def merge_stats(stats, axis):
    every = lax.all_gather(stats, axis, axis=0, tiled=False)
    top = jnp.max(every[:, 0], axis=0)
    shrink = jnp.exp(every[:, 0] - top[None])
    return jnp.stack(
        [
            top,
            jnp.sum(every[:, 1] * shrink, axis=0),
            jnp.sum(every[:, 2] * shrink, axis=0),
            jnp.sum(every[:, 3], axis=0),
        ]
    )


def per_device(
    hidden_in,
    state,
    attn_norm_gain,
    w_query,
    w_key,
    w_value,
    w_gate,
    w_decay,
    w_beta,
    decay_log,
    decay_bias,
    head_gain,
    w_out,
    final_gain,
    lm_weight,
    token_ids,
    ref_logprob,
):
    highest = lax.Precision.HIGHEST
    row_count = lax.axis_size("row")
    col_count = lax.axis_size("col")
    row_index = lax.axis_index("row")
    col_index = lax.axis_index("col")
    group = max(1, row_count // HEADS)
    local_heads = max(1, HEADS // row_count)
    first_head = row_index // group * local_heads
    value_cols = w_value.shape[1]
    value_part = value_cols // local_heads
    block_rows = hidden_in.shape[0]
    key_rows = state.shape[0]
    batch = state.shape[2]
    vocab_dev = lm_weight.shape[1]
    packed = jnp.concatenate([hidden_in, final_gain[None, :]], axis=0)
    whole = lax.all_gather(packed, "row", axis=1, tiled=True)
    whole_rows = whole[:block_rows]
    whole_gain = whole[block_rows].astype(jnp.float32)
    xfull = whole_rows.astype(jnp.float32)
    normed = (
        xfull
        * lax.rsqrt(jnp.mean(xfull * xfull, axis=1, keepdims=True) + 1e-06)
        * attn_norm_gain.astype(jnp.float32)
    ).astype(jnp.bfloat16)
    raw_pair = jnp.stack([project(w_query, normed), project(w_key, normed)]).astype(jnp.bfloat16)
    raw_pair = lax.optimization_barrier(raw_pair)
    for level in range(group.bit_length() - 1):
        partner = partner_2(raw_pair, "row", level)
        upper = row_index >> level & 1 == 1
        raw_pair = jnp.where(
            upper,
            jnp.concatenate([partner, raw_pair], axis=1),
            jnp.concatenate([raw_pair, partner], axis=1),
        )
    pair_f = raw_pair.astype(jnp.float32).reshape(2, local_heads, DK, block_rows)
    unit_pair = (
        pair_f * lax.rsqrt(jnp.sum(pair_f * pair_f, axis=2, keepdims=True) + 1e-06)
    ).astype(jnp.bfloat16)
    key_blocks = unit_pair.reshape(2, local_heads, col_count, key_rows, block_rows)
    swapped = swap_blocks(jnp.transpose(key_blocks, (2, 0, 1, 3, 4)), "col")
    tiles_qk = jnp.transpose(swapped, (1, 2, 3, 0, 4)).reshape(2, local_heads, key_rows, batch)
    query = tiles_qk[0].astype(jnp.float32)
    key = tiles_qk[1].astype(jnp.float32)
    unit_f = unit_pair.astype(jnp.float32)
    intersection = jnp.sum(unit_f[0] * unit_f[1], axis=1)
    value_t = project(w_value, normed)
    gate_t = project(w_gate, normed)
    decay_in = lax.dynamic_slice_in_dim(project(w_decay, normed), first_head, local_heads, 0)
    beta_in = lax.dynamic_slice_in_dim(project(w_beta, normed), first_head, local_heads, 0)
    rate = jnp.exp(lax.dynamic_slice_in_dim(decay_log, first_head, local_heads, 0))
    bias = lax.dynamic_slice_in_dim(decay_bias, first_head, local_heads, 0)
    alpha_t = jnp.exp(-rate[:, None] * jax.nn.softplus(decay_in + bias[:, None]))
    beta_t = jax.nn.sigmoid(beta_in)
    tiles = state.reshape(key_rows, local_heads, value_part, batch)
    value4 = value_t.reshape(local_heads, value_part, block_rows)
    key_major = jnp.transpose(key, (1, 0, 2))
    responses = jnp.stack(
        [
            jnp.einsum("khvb,hkb->hvb", tiles, key, precision=highest),
            jnp.einsum("khvb,hkb->hvb", tiles, query, precision=highest),
        ]
    )
    responses = responses.reshape(2, local_heads, value_part, col_count, block_rows)
    recall, answer = lax.psum_scatter(
        jnp.transpose(responses, (3, 0, 1, 2, 4)), "col", scatter_dimension=0, tiled=False
    )
    write = beta_t[:, None, :] * (value4 - alpha_t[:, None, :] * recall)
    parts = gather_blocks(
        jnp.concatenate([write.reshape(value_cols, block_rows), alpha_t], axis=0), "col"
    )
    parts = jnp.transpose(parts, (1, 0, 2)).reshape(value_cols + local_heads, batch)
    write_all = parts[:value_cols].reshape(local_heads, value_part, batch)
    alpha_all = parts[value_cols:]
    updated = alpha_all[None, :, None, :] * tiles + key_major[:, :, None, :] * write_all[None]
    readout = alpha_t[:, None, :] * answer + intersection[:, None, :] * write
    power = jnp.sum(readout * readout, axis=1)
    for level in range(group.bit_length() - 1):
        power = power + partner_2(power, "row", level)
    gain_part = lax.dynamic_slice_in_dim(head_gain, row_index % group * value_part, value_part, 0)
    gate4 = gate_t.reshape(local_heads, value_part, block_rows)
    mixed = (
        readout
        * lax.rsqrt(power / DV + 1e-05)[:, None, :]
        * gain_part[None, :, None]
        * jax.nn.silu(gate4)
    )
    mixed_heads = mixed.reshape(value_cols, block_rows).astype(jnp.bfloat16)
    share = -(-block_rows // row_count)
    extra = share * row_count - block_rows
    partial = lax.dot_general(
        mixed_heads, w_out, (((0,), (0,)), ((), ())), preferred_element_type=jnp.float32
    )
    branch = lax.psum_scatter(
        jnp.pad(partial, ((0, extra), (0, 0))).reshape(row_count, share, D),
        "row",
        scatter_dimension=0,
        tiled=False,
    )
    own_rows = lax.dynamic_slice_in_dim(
        jnp.pad(whole_rows, ((0, extra), (0, 0))), row_index * share, share, 0
    )
    hidden = own_rows.astype(jnp.float32) + branch
    energy = jnp.mean(hidden * hidden, axis=1, keepdims=True)
    final = (hidden * lax.rsqrt(energy + 1e-06) * whole_gain[None, :]).astype(jnp.bfloat16)
    tall = lax.all_gather(final, ("col", "row"), axis=0, tiled=True)
    if extra:
        tall = tall.reshape(col_count, share * row_count, D)[:, :block_rows].reshape(batch, D)
    logits = jnp.dot(tall, lm_weight, preferred_element_type=jnp.float32)
    vocab_start = (row_index * col_count + col_index) * vocab_dev
    hits = jnp.arange(vocab_dev, dtype=jnp.int32)[None, :] + vocab_start == token_ids[:, None]
    local_pick = jnp.sum(jnp.where(hits, logits, jnp.zeros_like(logits)), axis=1)
    local_top = jnp.max(logits, axis=1)
    expo = jnp.exp(logits - local_top[:, None])
    local_total = jnp.sum(expo, axis=1)
    local_weighted = jnp.sum(expo * logits, axis=1)
    stats = jnp.stack([local_top, local_total, local_weighted, local_pick])
    top, total, weighted, picked = merge_stats(merge_stats(stats, "col"), "row")
    lse = top + jnp.log(total)
    logprob = picked - lse
    entropy = lse - weighted / total
    gap = jnp.clip(ref_logprob - logprob, -20.0, 20.0)
    kl = jnp.minimum(jnp.exp(gap) - gap - 1.0, 10.0)
    new_state = updated.reshape(key_rows, value_cols, batch)
    return (new_state, logprob, entropy, kl)


def solution(mesh):
    in_specs = (
        P("col", "row"),
        P("col", "row", None),
        P(),
        P(None, "row"),
        P(None, "row"),
        P(None, "row"),
        P(None, "row"),
        P(),
        P(),
        P(),
        P(),
        P(),
        P("row", None),
        P("row"),
        P(None, ("row", "col")),
        P(),
        P(),
    )
    out_specs = (P("col", "row", None), P(), P(), P())
    return jax.shard_map(
        per_device, mesh=mesh, in_specs=in_specs, out_specs=out_specs, check_vma=False
    )
```

profile of v0, /device:TPU:0, one launch (start us, length us, event | category | flops | bytes accessed | tf_op | source)
XLA Modules:
  0.0 320.8 jit_solution(1117575225942106937)
XLA Ops:
  8.0 1.6 pad_maximum_fusion.1
  10.5 26.9 %all-gather.8.cloned.1.call-done = bf16[289,2048]{1,0:T(8,128)(2,1)} async-done(((bf16[289,256]{1,0:T(8,128)(2,1)}), bf16[289,2048]{1,0:T(8,128)(2,1)}) %all-gather.8.cloned.1.call-update) | async-done | bytes 1183760 | tf_op jit(solution)/shard_map/all_gather | solution.py:112
  37.4 1.7 fusion.2
  39.1 1.6 fusion.4
  45.9 2.5 multiply_reduce_fusion.3
  51.2 2.4 collective-permute-start.2
  54.2 2.9 collective-permute-done
  57.1 5.6 %collective-permute-done.1 = bf16[1,2,2,32,288]{4,3,0,2,1:T(8,128)(2,1)S(1)} collective-permute-done((bf16[1,2,2,32,288]{4,3,0,2,1:T(8,128)(2,1)S(1)}, bf16[1,2,2,32,288]{4,3,0,2,1:T(8,128)(2,1)S(1)}, u32[]{:S(2)}, u32[]{:S(2)}) %collective-permute-start.1) | collective-permute-done | bytes 73760 | tf_op jit(solution)/shard_map/ppermute | solution.py:38
  64.6 17.3 %multiply_reduce_fusion.1 = (f32[2,1152,128]{1,2,0:T(8,128)}, f32[2,1152,128]{1,2,0:T(8,128)}) fusion(f32[2,1152,32,128]{1,3,0,2:T(8,128)} %bitcast.222, f32[2,1152,32]{1,0,2:T(2,128)S(1)} %copy.148, f32[2,1152,32]{1,0,2:T(2,128)S(1)} %copy.149), kind=kLoop, calls=%fused_computation.3 | loop fusion | flops 37158912 | bytes 40697856
  81.9 2.6 copy.130
  84.6 2.7 copy.138
  87.2 1.8 maximum_bitcast_fusion
  89.0 1.6 copy.107
  92.3 1.7 fusion.53
  94.3 2.0 fusion.52
  97.1 1.7 fusion.9
  99.3 37.5 %reduce-scatter.3.cloned.1.call-done = f32[1,2,2,128,288]{3,4,2,1,0:T(8,128)} async-done(((f32[4,2,2,128,288]{3,4,2,1,0:T(8,128)}), f32[1,2,2,128,288]{3,4,2,1,0:T(8,128)}) %reduce-scatter.3.cloned.1.call-update) | async-done | bytes 589840 | tf_op jit(solution)/shard_map/reduce_scatter | solution.py:160
  142.5 2.2 fusion.22
  144.8 3.2 %fusion.7 = f32[8,36,2048]{2,1,0:T(8,128)} fusion(bf16[8,36,256]{2,1,0:T(8,128)(2,1)S(1)} %dot_general.55, bf16[256,2048]{1,0:T(8,128)(2,1)} %param.29), kind=kOutput, calls=%fused_computation.19 | convolution fusion | flops 301989888 | bytes 3555328 | tf_op jit(solution)/shard_map/dot_general | solution.py:186
  148.1 2.5 slice.72
  151.4 39.7 %reduce-scatter.5.cloned.1.call-done = f32[1,36,2048]{2,1,0:T(8,128)} async-done(((f32[8,36,2048]{2,1,0:T(8,128)}), f32[1,36,2048]{2,1,0:T(8,128)}) %reduce-scatter.5.cloned.1.call-update) | async-done | bytes 294928 | tf_op jit(solution)/shard_map/reduce_scatter | solution.py:189
  192.3 1.8 fusion.23
  196.3 2.4 collective-permute-start.4
  201.3 10.6 %collective-permute-done.3 = f32[1,258,288]{1,2,0:T(8,128)} collective-permute-done((f32[1,258,288]{1,2,0:T(8,128)}, f32[1,258,288]{1,2,0:T(8,128)}, u32[]{:S(2)}, u32[]{:S(2)}) %collective-permute-start.3) | collective-permute-done | bytes 297248 | tf_op jit(solution)/shard_map/ppermute | solution.py:49
  212.9 18.4 %collective-permute-done.4 = f32[1,258,288]{1,2,0:T(8,128)} collective-permute-done((f32[1,258,288]{1,2,0:T(8,128)}, f32[1,258,288]{1,2,0:T(8,128)}, u32[]{:S(2)}, u32[]{:S(2)}) %collective-permute-start.4) | collective-permute-done | bytes 297248 | tf_op jit(solution)/shard_map/ppermute | solution.py:49
  233.6 2.7 copy.112
  237.8 28.8 %fusion = f32[32,256,1152]{2,1,0:T(8,128)} fusion(f32[32,256,1152]{2,1,0:T(8,128)} %param.18, f32[256,1152]{1,0:T(8,128)S(1)} %copy-done.4, f32[32,2,1152]{2,1,0:T(2,128)S(1)} %copy-done.8, f32[256,1152]{1,0:T(8,128)S(1)} %bitcast.230), kind=kLoop, calls=%fused_computation.1 | loop fusion | flops 28311552 | bytes 78151680 | tf_op jit(solution)/shard_map/add | solution.py:170
  266.6 9.4 %all-gather.10.cloned.1.call-done = bf16[32,36,2048]{2,1,0:T(8,128)(2,1)} async-done(((bf16[1,36,2048]{2,1,0:T(8,128)(2,1)}), bf16[32,36,2048]{2,1,0:T(8,128)(2,1)}) %all-gather.10.cloned.1.call-update) | async-done | bytes 4718608 | tf_op jit(solution)/shard_map/all_gather | solution.py:201
  276.0 7.2 %reshape.120 = bf16[1152,2048]{1,0:T(8,128)(2,1)} reshape(bf16[32,36,2048]{2,1,0:T(8,128)(2,1)} %all-gather.10.cloned.1.call-done) | data formatting | bytes 9437184
  283.2 6.2 %fusion.51 = (f32[1152]{0:T(1024)S(1)}, f32[1152,640]{0,1:T(8,128)S(1)}) fusion(bf16[1152,2048]{1,0:T(8,128)(2,1)} %reshape.120, bf16[2048,640]{1,0:T(8,128)(2,1)S(1)} %copy-done), kind=kOutput, calls=%fused_computation.118 | convolution fusion | flops 3020635136 | bytes 10293760 | tf_op jit(solution)/shard_map/dot_general | solution.py:204
  290.5 13.5 %all-gather.3 = f32[4,4,1152]{2,1,0:T(4,128)S(1)} all-gather(f32[1,4,1152]{2,1,0:T(4,128)S(1)} %maximum_bitcast_fusion.2), channel_id=2, replica_groups=mesh['row'=8,'col'=4] {'col'}, dimensions={0}, use_global_device_ids=true | all-gather | bytes 92160 | tf_op jit(solution)/shard_map/all_gather | solution.py:65
  304.1 9.4 %all-gather.4 = f32[8,4,1152]{2,1,0:T(4,128)S(1)} all-gather(f32[1,4,1152]{2,1,0:T(4,128)S(1)} %maximum_bitcast_fusion.3), channel_id=3, replica_groups=mesh['row'=8,'col'=4] {'row'}, dimensions={0}, use_global_device_ids=true | all-gather | bytes 165888 | tf_op jit(solution)/shard_map/all_gather | solution.py:65
  (134 shorter events, 34.4 us)
Async XLA Ops:
  7.2 276.1 %copy-start = (bf16[2048,640]{1,0:T(8,128)(2,1)S(1)}, bf16[2048,640]{1,0:T(8,128)(2,1)}, u32[]{:S(2)}) copy-start(bf16[2048,640]{1,0:T(8,128)(2,1)} %param.31) | copy-start | bytes 7864324
  7.2 30.2 %all-gather.8.cloned.1.call-start = ((), (), s32[]{:S(2)}) async-start(), calls=%async_computation.2 | async-start | bytes 1363968 | tf_op jit(solution)/shard_map/all_gather | solution.py:112
  9.6 127.2 %reduce-scatter.3.cloned.1.call-start = ((), (), s32[]{:S(2)}) async-start(), calls=%async_computation.3 | async-start | bytes 2949120 | tf_op jit(solution)/shard_map/reduce_scatter | solution.py:160
  37.4 3.3 %copy-start.16 = (bf16[2048,256]{1,0:T(8,128)(2,1)S(1)}, bf16[2048,256]{1,0:T(8,128)(2,1)}, u32[]{:S(2)}) copy-start(bf16[2048,256]{1,0:T(8,128)(2,1)} %param.21) | copy-start | bytes 3145732
  40.7 1.1 copy-start.1
  40.7 1.7 copy-start.17
  42.9 0.7 copy-start.5
  49.6 7.5 %collective-permute-start = (bf16[1,2,2,32,288]{4,3,0,2,1:T(8,128)(2,1)S(1)}, bf16[1,2,2,32,288]{4,3,0,2,1:T(8,128)(2,1)S(1)}, u32[]{:S(2)}, u32[]{:S(2)}) collective-permute-start(bf16[1,2,2,32,288]{4,3,0,2,1:T(8,128)(2,1)S(1)} %get-tuple-element.25), channel_id=1, source_target_pairs={{0,1},{1,2},{2,3},{3,0},{4,5},{5,6},{6,7},{7,4},{8,9},{9,10},{10,1... | collective-permute-start | bytes 221192 | tf_op jit(solution)/shard_map/ppermute | solution.py:38
  51.2 11.5 %collective-permute-start.2 = (bf16[1,2,2,32,288]{4,3,0,2,1:T(8,128)(2,1)S(1)}, bf16[1,2,2,32,288]{4,3,0,2,1:T(8,128)(2,1)S(1)}, u32[]{:S(2)}, u32[]{:S(2)}) collective-permute-start(bf16[1,2,2,32,288]{4,3,0,2,1:T(8,128)(2,1)S(1)} %get-tuple-element.23), channel_id=1, source_target_pairs={{0,3},{1,0},{2,1},{3,2},{4,7},{5,4},{6,5},{7,6},{8,11},{9,8},{10,9... | collective-permute-start | bytes 221192 | tf_op jit(solution)/shard_map/ppermute | solution.py:38
  53.6 9.1 %collective-permute-start.1 = (bf16[1,2,2,32,288]{4,3,0,2,1:T(8,128)(2,1)S(1)}, bf16[1,2,2,32,288]{4,3,0,2,1:T(8,128)(2,1)S(1)}, u32[]{:S(2)}, u32[]{:S(2)}) collective-permute-start(bf16[1,2,2,32,288]{4,3,0,2,1:T(8,128)(2,1)S(1)} %get-tuple-element.24), channel_id=1, source_target_pairs={{0,2},{1,3},{2,0},{3,1},{4,6},{5,7},{6,4},{7,5},{8,10},{9,11},{10,... | collective-permute-start | bytes 221192 | tf_op jit(solution)/shard_map/ppermute | solution.py:38
  90.6 0.7 copy-start.18
  90.6 0.7 copy-start.19
  90.6 0.8 copy-start.20
  90.6 1.7 copy-start.12
  90.6 3.7 %copy-start.13 = (bf16[2048,16]{0,1:T(8,128)(2,1)S(1)}, bf16[2048,16]{0,1:T(8,128)(2,1)}, u32[]{:S(2)}) copy-start(bf16[2048,16]{0,1:T(8,128)(2,1)} %param.25) | copy-start | bytes 196612
  90.6 6.5 %copy-start.3 = (f32[2,2,128,288]{2,1,3,0:T(2,128)S(1)}, f32[2,2,128,288]{2,1,3,0:T(2,128)}, u32[]{:S(2)}) copy-start(f32[2,2,128,288]{2,1,3,0:T(2,128)} %reshape.113) | copy-start | bytes 1769476
  90.7 100.4 %reduce-scatter.5.cloned.1.call-start = ((), (), s32[]{:S(2)}) async-start(), calls=%async_computation.4 | async-start | bytes 2949120 | tf_op jit(solution)/shard_map/reduce_scatter | solution.py:189
  98.8 40.4 %copy-start.11 = (f32[2,288]{0,1:T(8,128)S(1)}, f32[2,288]{0,1:T(8,128)}, u32[]{:S(2)}) copy-start(f32[2,288]{0,1:T(8,128)} %copy.146) | copy-start | bytes 6916
  136.8 3.2 copy-start.2
  136.8 3.2 copy-start.10
  140.0 0.7 copy-start.7
  140.0 1.2 copy-start.6
  148.0 128.0 %all-gather.10.cloned.1.call-start = ((), (), s32[]{:S(2)}) async-start(), calls=%async_computation.5 | async-start | bytes 5406720 | tf_op jit(solution)/shard_map/all_gather | solution.py:201
  148.1 50.7 %copy-start.9 = (f32[32,2,1152]{2,0,1:T(8,128)S(1)}, f32[32,2,1152]{2,0,1:T(8,128)}, u32[]{:S(2)}) copy-start(f32[32,2,1152]{2,0,1:T(8,128)} %get-tuple-element.31) | copy-start | bytes 884740
  194.9 17.0 %collective-permute-start.3 = (f32[1,258,288]{1,2,0:T(8,128)}, f32[1,258,288]{1,2,0:T(8,128)}, u32[]{:S(2)}, u32[]{:S(2)}) collective-permute-start(f32[1,258,288]{1,2,0:T(8,128)} %maximum_bitcast_fusion.1), channel_id=1, source_target_pairs={{0,1},{1,2},{2,3},{3,0},{4,5},{5,6},{6,7},{7,4},{8,9},{9,10},{10,1... | collective-permute-start | bytes 891656 | tf_op jit(solution)/shard_map/ppermute | solution.py:49
  196.3 35.0 %collective-permute-start.4 = (f32[1,258,288]{1,2,0:T(8,128)}, f32[1,258,288]{1,2,0:T(8,128)}, u32[]{:S(2)}, u32[]{:S(2)}) collective-permute-start(f32[1,258,288]{1,2,0:T(8,128)} %maximum_bitcast_fusion.1), channel_id=1, source_target_pairs={{0,2},{1,3},{2,0},{3,1},{4,6},{5,7},{6,4},{7,5},{8,10},{9,11},{10,... | collective-permute-start | bytes 891656 | tf_op jit(solution)/shard_map/ppermute | solution.py:49
  199.7 32.6 %collective-permute-start.5 = (f32[1,258,288]{1,2,0:T(8,128)}, f32[1,258,288]{1,2,0:T(8,128)S(1)}, u32[]{:S(2)}, u32[]{:S(2)}) collective-permute-start(f32[1,258,288]{1,2,0:T(8,128)} %maximum_bitcast_fusion.1), channel_id=1, source_target_pairs={{0,3},{1,0},{2,1},{3,2},{4,7},{5,4},{6,5},{7,6},{8,11},{9,8},{10,9... | collective-permute-start | bytes 891656 | tf_op jit(solution)/shard_map/ppermute | solution.py:49
  233.6 3.0 copy-start.8
  236.5 1.3 copy-start.4
  283.2 6.2 %copy-start.14 = (s32[1152]{0:T(1024)S(1)}, s32[1152]{0:T(1024)}, u32[]{:S(2)}) copy-start(s32[1152]{0:T(1024)} %param.32) | copy-start | bytes 13828
  289.5 24.2 %copy-start.15 = (f32[1152]{0:T(1024)S(1)}, f32[1152]{0:T(1024)}, u32[]{:S(2)}) copy-start(f32[1152]{0:T(1024)} %param.33) | copy-start | bytes 13828
Sparse Core Ops, SparseCore 0:
  10.4 26.9 all-gather.7
  90.8 45.9 reduce-scatter.2
  148.2 42.8 reduce-scatter.4
  194.2 81.7 all-gather.9
where the time goes:
time: 322 us; the launch traced here: 321 us
  waiting for transfers between devices  151 us (47%)
  other arithmetic  66.1 us (21%)
  local copies, waits for them, and re-layouts  39.7 us (12%)
  blocking collectives  22.8 us (7%)
  matrix products  16.8 us (5%)
  between operations  14.4 us (4%)
  starting transfers between devices  10 us (3%)
    reduce_scatter x1, waiting for transfers between devices, per_device(): lax.psum_scatter(jnp.pad(partial, ((0, extra), (0, 0))).reshape(row_count...  39.7 us
    reduce_scatter x1, waiting for transfers between devices, per_device(): lax.psum_scatter(jnp.transpose(responses, (3, 0, 1, 2, 4)), 'col', scatte...  37.5 us
    ppermute x3, waiting for transfers between devices, gather_blocks(): got = lax.ppermute(block[None], axis, shift_pairs(count, step))  29 us
    add x1, other arithmetic, per_device(): alpha_all[None, :, None, :] * tiles  28.8 us
    all_gather x1, waiting for transfers between devices, per_device(): whole = lax.all_gather(packed, 'row', axis=1, tiled=True)  26.9 us
    all_gather x2, blocking collectives, merge_stats(): every = lax.all_gather(stats, axis, axis=0, tiled=False)  22.8 us
    unnamed x5, other arithmetic  19.2 us
    unnamed x47, local copies, waits for them, and re-layouts  13 us
  transfers between devices with their start and end apart: 10, of which 8 were waited for; matrix products, arithmetic and copies ran while one was open for 15% of the time, Pallas kernels for 0%

commit v1 on v0

--- a/solution.py
+++ b/solution.py
@@ -109,7 +109,7 @@
     batch = state.shape[2]
     vocab_dev = lm_weight.shape[1]
     packed = jnp.concatenate([hidden_in, final_gain[None, :]], axis=0)
-    whole = lax.all_gather(packed, "row", axis=1, tiled=True)
+    whole = jnp.concatenate(lax.all_gather(packed, "row"), axis=1)
     whole_rows = whole[:block_rows]
     whole_gain = whole[block_rows].astype(jnp.float32)
     xfull = whole_rows.astype(jnp.float32)

time: 322 us -> 324 us (level)
    unnamed x47 -> x50, local copies, waits for them, and re-layouts: 13 us -> 15.6 us
    unnamed x5 -> x6, other arithmetic: 19.2 us -> 20.7 us
  transfers between devices with their start and end apart: 10 -> 10, of which waited for: 8 -> 8; matrix products, arithmetic and copies ran while one was open for 15% -> 14% of each run, Pallas kernels for 0% -> 0%
where the time goes in v1:
time: 324 us; the launch traced here: 322 us
  waiting for transfers between devices  153 us (47%)
  other arithmetic  64.8 us (20%)
  local copies, waits for them, and re-layouts  40 us (12%)
  blocking collectives  22.8 us (7%)
  matrix products  16.7 us (5%)
  between operations  14.4 us (4%)
  starting transfers between devices  10 us (3%)
    reduce_scatter x1, waiting for transfers between devices, per_device(): lax.psum_scatter(jnp.pad(partial, ((0, extra), (0, 0))).reshape(row_count...  42.2 us
    reduce_scatter x1, waiting for transfers between devices, per_device(): lax.psum_scatter(jnp.transpose(responses, (3, 0, 1, 2, 4)), 'col', scatte...  37.5 us
    ppermute x3, waiting for transfers between devices, gather_blocks(): got = lax.ppermute(block[None], axis, shift_pairs(count, step))  28.9 us
    add x1, other arithmetic, per_device(): alpha_all[None, :, None, :] * tiles  28.8 us
    all_gather x1, waiting for transfers between devices, per_device(): whole = jnp.concatenate(lax.all_gather(packed, 'row'), axis=1)  26.8 us
    all_gather x2, blocking collectives, merge_stats(): every = lax.all_gather(stats, axis, axis=0, tiled=False)  22.8 us
    unnamed x6, other arithmetic  20.7 us
    unnamed x50, local copies, waits for them, and re-layouts  15.6 us
  transfers between devices with their start and end apart: 10, of which 8 were waited for; matrix products, arithmetic and copies ran while one was open for 14% of the time, Pallas kernels for 0%

profile of v1, /device:TPU:0, one launch (start us, length us, event | category | flops | bytes accessed | tf_op | source)
XLA Modules:
  0.0 322.2 jit_solution(15305132336633405148)
XLA Ops:
  8.0 1.6 maximum_bitcast_fusion.2
  10.5 26.8 %all-gather.10.cloned.1.call-done = bf16[8,289,256]{2,1,0:T(8,128)(2,1)} async-done(((bf16[1,289,256]{2,1,0:T(8,128)(2,1)}), bf16[8,289,256]{2,1,0:T(8,128)(2,1)}) %all-gather.10.cloned.1.call-update) | async-done | bytes 1183760 | tf_op jit(solution)/shard_map/all_gather | solution.py:112
  37.3 1.6 multiply_reduce_fusion.3
  47.2 2.5 multiply_reduce_fusion.4
  50.9 1.5 collective-permute-start
  52.5 2.4 collective-permute-start.2
  55.5 2.9 collective-permute-done
  58.4 5.6 %collective-permute-done.1 = bf16[1,2,2,32,288]{4,3,0,2,1:T(8,128)(2,1)S(1)} collective-permute-done((bf16[1,2,2,32,288]{4,3,0,2,1:T(8,128)(2,1)S(1)}, bf16[1,2,2,32,288]{4,3,0,2,1:T(8,128)(2,1)S(1)}, u32[]{:S(2)}, u32[]{:S(2)}) %collective-permute-start.1) | collective-permute-done | bytes 73760 | tf_op jit(solution)/shard_map/ppermute | solution.py:38
  65.9 17.3 %multiply_reduce_fusion.1 = (f32[2,1152,128]{1,2,0:T(8,128)}, f32[2,1152,128]{1,2,0:T(8,128)}) fusion(f32[2,1152,32,128]{1,3,0,2:T(8,128)} %bitcast.228, f32[2,1152,32]{1,0,2:T(2,128)S(1)} %copy.154, f32[2,1152,32]{1,0,2:T(2,128)S(1)} %copy.155), kind=kLoop, calls=%fused_computation.3 | loop fusion | flops 37158912 | bytes 40697856
  83.2 2.7 copy.136
  85.9 2.7 copy.144
  88.6 1.8 maximum_bitcast_fusion
  90.4 1.6 copy.113
  93.6 1.7 fusion.50
  95.6 2.0 fusion.49
  98.4 1.7 fusion.6
  100.6 37.5 %reduce-scatter.3.cloned.1.call-done = f32[1,2,2,128,288]{3,4,2,1,0:T(8,128)} async-done(((f32[4,2,2,128,288]{3,4,2,1,0:T(8,128)}), f32[1,2,2,128,288]{3,4,2,1,0:T(8,128)}) %reduce-scatter.3.cloned.1.call-update) | async-done | bytes 589840 | tf_op jit(solution)/shard_map/reduce_scatter | solution.py:160
  143.8 2.2 fusion.19
  146.1 3.2 %fusion.4 = f32[8,36,2048]{2,1,0:T(8,128)} fusion(bf16[8,36,256]{2,1,0:T(8,128)(2,1)S(1)} %dot_general.55, bf16[256,2048]{1,0:T(8,128)(2,1)} %param.29), kind=kOutput, calls=%fused_computation.16 | convolution fusion | flops 301989888 | bytes 3555328 | tf_op jit(solution)/shard_map/dot_general | solution.py:186
  150.2 42.2 %reduce-scatter.5.cloned.1.call-done = f32[1,36,2048]{2,1,0:T(8,128)} async-done(((f32[8,36,2048]{2,1,0:T(8,128)}), f32[1,36,2048]{2,1,0:T(8,128)}) %reduce-scatter.5.cloned.1.call-update) | async-done | bytes 294928 | tf_op jit(solution)/shard_map/reduce_scatter | solution.py:189
  193.6 1.8 fusion.20
  196.2 1.5 collective-permute-start.3
  197.7 2.4 collective-permute-start.4
  202.6 10.5 %collective-permute-done.3 = f32[1,258,288]{1,2,0:T(8,128)} collective-permute-done((f32[1,258,288]{1,2,0:T(8,128)}, f32[1,258,288]{1,2,0:T(8,128)}, u32[]{:S(2)}, u32[]{:S(2)}) %collective-permute-start.3) | collective-permute-done | bytes 297248 | tf_op jit(solution)/shard_map/ppermute | solution.py:49
  214.2 18.4 %collective-permute-done.4 = f32[1,258,288]{1,2,0:T(8,128)} collective-permute-done((f32[1,258,288]{1,2,0:T(8,128)}, f32[1,258,288]{1,2,0:T(8,128)}, u32[]{:S(2)}, u32[]{:S(2)}) %collective-permute-start.4) | collective-permute-done | bytes 297248 | tf_op jit(solution)/shard_map/ppermute | solution.py:49
  234.9 2.7 copy.118
  239.1 28.8 %fusion = f32[32,256,1152]{2,1,0:T(8,128)} fusion(f32[32,256,1152]{2,1,0:T(8,128)} %param.18, f32[256,1152]{1,0:T(8,128)S(1)} %copy-done.5, f32[32,2,1152]{2,1,0:T(2,128)S(1)} %copy-done.9, f32[256,1152]{1,0:T(8,128)S(1)} %bitcast.239), kind=kLoop, calls=%fused_computation.1 | loop fusion | flops 28311552 | bytes 78151680 | tf_op jit(solution)/shard_map/add | solution.py:170
  267.9 9.4 %all-gather.12.cloned.1.call-done = bf16[32,36,2048]{2,1,0:T(8,128)(2,1)} async-done(((bf16[1,36,2048]{2,1,0:T(8,128)(2,1)}), bf16[32,36,2048]{2,1,0:T(8,128)(2,1)}) %all-gather.12.cloned.1.call-update) | async-done | bytes 4718608 | tf_op jit(solution)/shard_map/all_gather | solution.py:201
  277.3 7.2 %reshape.138 = bf16[1152,2048]{1,0:T(8,128)(2,1)} reshape(bf16[32,36,2048]{2,1,0:T(8,128)(2,1)} %all-gather.12.cloned.1.call-done) | data formatting | bytes 9437184
  284.6 6.2 %fusion.48 = (f32[1152]{0:T(1024)S(1)}, f32[1152,640]{0,1:T(8,128)S(1)}) fusion(bf16[1152,2048]{1,0:T(8,128)(2,1)} %reshape.138, bf16[2048,640]{1,0:T(8,128)(2,1)S(1)} %copy-done), kind=kOutput, calls=%fused_computation.116 | convolution fusion | flops 3020635136 | bytes 10293760 | tf_op jit(solution)/shard_map/dot_general | solution.py:204
  291.8 13.5 %all-gather.5 = f32[4,4,1152]{2,1,0:T(4,128)S(1)} all-gather(f32[1,4,1152]{2,1,0:T(4,128)S(1)} %maximum_bitcast_fusion.3), channel_id=3, replica_groups=mesh['row'=8,'col'=4] {'col'}, dimensions={0}, use_global_device_ids=true | all-gather | bytes 92160 | tf_op jit(solution)/shard_map/all_gather | solution.py:65
  305.5 9.3 %all-gather.6 = f32[8,4,1152]{2,1,0:T(4,128)S(1)} all-gather(f32[1,4,1152]{2,1,0:T(4,128)S(1)} %maximum_bitcast_fusion.4), channel_id=4, replica_groups=mesh['row'=8,'col'=4] {'row'}, dimensions={0}, use_global_device_ids=true | all-gather | bytes 165888 | tf_op jit(solution)/shard_map/all_gather | solution.py:65
  (137 shorter events, 34.6 us)
Async XLA Ops:
  7.2 277.4 %copy-start = (bf16[2048,640]{1,0:T(8,128)(2,1)S(1)}, bf16[2048,640]{1,0:T(8,128)(2,1)}, u32[]{:S(2)}) copy-start(bf16[2048,640]{1,0:T(8,128)(2,1)} %param.31) | copy-start | bytes 7864324
  7.2 30.1 %all-gather.10.cloned.1.call-start = ((), (), s32[]{:S(2)}) async-start(), calls=%async_computation.4 | async-start | bytes 1363968 | tf_op jit(solution)/shard_map/all_gather | solution.py:112
  9.6 128.5 %reduce-scatter.3.cloned.1.call-start = ((), (), s32[]{:S(2)}) async-start(), calls=%async_computation.2 | async-start | bytes 2949120 | tf_op jit(solution)/shard_map/reduce_scatter | solution.py:160
  40.4 2.2 copy-start.3
  40.4 1.7 copy-start.17
  42.0 1.0 copy-start.1
  42.0 1.7 copy-start.18
  44.2 0.7 copy-start.6
  50.9 7.5 %collective-permute-start = (bf16[1,2,2,32,288]{4,3,0,2,1:T(8,128)(2,1)S(1)}, bf16[1,2,2,32,288]{4,3,0,2,1:T(8,128)(2,1)S(1)}, u32[]{:S(2)}, u32[]{:S(2)}) collective-permute-start(bf16[1,2,2,32,288]{4,3,0,2,1:T(8,128)(2,1)S(1)} %get-tuple-element.25), channel_id=1, source_target_pairs={{0,1},{1,2},{2,3},{3,0},{4,5},{5,6},{6,7},{7,4},{8,9},{9,10},{10,1... | collective-permute-start | bytes 221192 | tf_op jit(solution)/shard_map/ppermute | solution.py:38
  52.5 11.5 %collective-permute-start.2 = (bf16[1,2,2,32,288]{4,3,0,2,1:T(8,128)(2,1)S(1)}, bf16[1,2,2,32,288]{4,3,0,2,1:T(8,128)(2,1)S(1)}, u32[]{:S(2)}, u32[]{:S(2)}) collective-permute-start(bf16[1,2,2,32,288]{4,3,0,2,1:T(8,128)(2,1)S(1)} %get-tuple-element.23), channel_id=1, source_target_pairs={{0,3},{1,0},{2,1},{3,2},{4,7},{5,4},{6,5},{7,6},{8,11},{9,8},{10,9... | collective-permute-start | bytes 221192 | tf_op jit(solution)/shard_map/ppermute | solution.py:38
  54.9 9.1 %collective-permute-start.1 = (bf16[1,2,2,32,288]{4,3,0,2,1:T(8,128)(2,1)S(1)}, bf16[1,2,2,32,288]{4,3,0,2,1:T(8,128)(2,1)S(1)}, u32[]{:S(2)}, u32[]{:S(2)}) collective-permute-start(bf16[1,2,2,32,288]{4,3,0,2,1:T(8,128)(2,1)S(1)} %get-tuple-element.24), channel_id=1, source_target_pairs={{0,2},{1,3},{2,0},{3,1},{4,6},{5,7},{6,4},{7,5},{8,10},{9,11},{10,... | collective-permute-start | bytes 221192 | tf_op jit(solution)/shard_map/ppermute | solution.py:38
  91.9 0.7 copy-start.19
  91.9 0.7 copy-start.20
  91.9 0.8 copy-start.21
  91.9 1.7 copy-start.13
  91.9 3.6 %copy-start.14 = (bf16[2048,16]{0,1:T(8,128)(2,1)S(1)}, bf16[2048,16]{0,1:T(8,128)(2,1)}, u32[]{:S(2)}) copy-start(bf16[2048,16]{0,1:T(8,128)(2,1)} %param.25) | copy-start | bytes 196612
  92.0 6.5 %copy-start.4 = (f32[2,2,128,288]{2,1,3,0:T(2,128)S(1)}, f32[2,2,128,288]{2,1,3,0:T(2,128)}, u32[]{:S(2)}) copy-start(f32[2,2,128,288]{2,1,3,0:T(2,128)} %reshape.128) | copy-start | bytes 1769476
  92.0 100.4 %reduce-scatter.5.cloned.1.call-start = ((), (), s32[]{:S(2)}) async-start(), calls=%async_computation.3 | async-start | bytes 2949120 | tf_op jit(solution)/shard_map/reduce_scatter | solution.py:189
  100.1 40.4 %copy-start.12 = (f32[2,288]{0,1:T(8,128)S(1)}, f32[2,288]{0,1:T(8,128)}, u32[]{:S(2)}) copy-start(f32[2,288]{0,1:T(8,128)} %copy.152) | copy-start | bytes 6916
  138.1 3.2 copy-start.2
  138.1 3.2 copy-start.11
  141.3 0.7 copy-start.8
  141.3 1.2 copy-start.7
  149.3 50.7 %copy-start.10 = (f32[32,2,1152]{2,0,1:T(8,128)S(1)}, f32[32,2,1152]{2,0,1:T(8,128)}, u32[]{:S(2)}) copy-start(f32[32,2,1152]{2,0,1:T(8,128)} %get-tuple-element.31) | copy-start | bytes 884740
  149.3 128.0 %all-gather.12.cloned.1.call-start = ((), (), s32[]{:S(2)}) async-start(), calls=%async_computation.5 | async-start | bytes 5406720 | tf_op jit(solution)/shard_map/all_gather | solution.py:201
  196.2 17.0 %collective-permute-start.3 = (f32[1,258,288]{1,2,0:T(8,128)}, f32[1,258,288]{1,2,0:T(8,128)}, u32[]{:S(2)}, u32[]{:S(2)}) collective-permute-start(f32[1,258,288]{1,2,0:T(8,128)} %maximum_bitcast_fusion.1), channel_id=1, source_target_pairs={{0,1},{1,2},{2,3},{3,0},{4,5},{5,6},{6,7},{7,4},{8,9},{9,10},{10,1... | collective-permute-start | bytes 891656 | tf_op jit(solution)/shard_map/ppermute | solution.py:49
  197.7 34.9 %collective-permute-start.4 = (f32[1,258,288]{1,2,0:T(8,128)}, f32[1,258,288]{1,2,0:T(8,128)}, u32[]{:S(2)}, u32[]{:S(2)}) collective-permute-start(f32[1,258,288]{1,2,0:T(8,128)} %maximum_bitcast_fusion.1), channel_id=1, source_target_pairs={{0,2},{1,3},{2,0},{3,1},{4,6},{5,7},{6,4},{7,5},{8,10},{9,11},{10,... | collective-permute-start | bytes 891656 | tf_op jit(solution)/shard_map/ppermute | solution.py:49
  201.0 32.6 %collective-permute-start.5 = (f32[1,258,288]{1,2,0:T(8,128)}, f32[1,258,288]{1,2,0:T(8,128)S(1)}, u32[]{:S(2)}, u32[]{:S(2)}) collective-permute-start(f32[1,258,288]{1,2,0:T(8,128)} %maximum_bitcast_fusion.1), channel_id=1, source_target_pairs={{0,3},{1,0},{2,1},{3,2},{4,7},{5,4},{6,5},{7,6},{8,11},{9,8},{10,9... | collective-permute-start | bytes 891656 | tf_op jit(solution)/shard_map/ppermute | solution.py:49
  234.9 3.0 copy-start.9
  237.8 1.3 copy-start.5
  284.6 6.2 %copy-start.15 = (s32[1152]{0:T(1024)S(1)}, s32[1152]{0:T(1024)}, u32[]{:S(2)}) copy-start(s32[1152]{0:T(1024)} %param.32) | copy-start | bytes 13828
  290.8 24.2 %copy-start.16 = (f32[1152]{0:T(1024)S(1)}, f32[1152]{0:T(1024)}, u32[]{:S(2)}) copy-start(f32[1152]{0:T(1024)} %param.33) | copy-start | bytes 13828
Sparse Core Ops, SparseCore 0:
  10.4 26.7 all-gather.9
  92.1 45.9 reduce-scatter.2
  149.5 42.8 reduce-scatter.4
  195.5 81.7 all-gather.11
